TPU v7x, 32 devices: a whole 2x2x4 slice. The times are simulated.
32 devices in a mesh: gx: 2 (over y), gy: 4 (over x, core), gz: 4 (over z).
Axes of the slice: x: 2, y: 2, z: 4, core: 2. Of those that a mesh axis runs over, the one named last changes fastest.
Arguments:
- velocity: float32 [3, 64, 128, 512], P(None, 'gx', 'gy', 'gz'), may hold values from -3 to 3
- box_level: float32 [512, 16, 256], P(('gx', 'gy', 'gz')), may hold values from -9 to 9
- corners: int32 [512, 3], P(('gx', 'gy', 'gz')), may hold values from 0 to 112, as said below
- owner_list: int32 [512], P(('gx', 'gy', 'gz')), may hold values from -1 to 15, as said below
Outputs:
- new_velocity: float32 [3, 64, 128, 512], P(None, 'gx', 'gy', 'gz')
- level_sets: float32 [512, 16, 256], P(('gx', 'gy', 'gz'))
- curvature: float32 [512, 16, 256], P(('gx', 'gy', 'gz'))
Inputs may be any that keep to these rules, and one draw needn't show every extreme that they name: `owner_list`: -1 marks an empty slot. The live slots of one device name different helpers, numbered in the order of the devices of its gy+gz group (gy slowest) at the device's own index along gx; every helper is named by exactly 8 slots of its group; a device has 0 to 16 live slots, and some device of every group has 16. `corners`: columns 0, 1, 2 lie in 0 to 16, 16, 112: every box lies inside its home device's block. Boxes may intersect.
All inputs are finite; a program needn't handle non-finite values.
Results may differ from a plain program's by a relative error of at most 0.0003.
Values sent between devices are 32-bit elements; how exact they have to be, the bound alone decides.
A program may use at most 128 MiB of HBM per device.

v0:
```python
import math

import jax
import jax.numpy as jnp
from jax import lax
from jax.sharding import PartitionSpec as P

ITERS = 12


box_step = 0.25
pseudo_step = 0.3
weno_floor = 1e-06
band_width = 1.5
tension = 2.0
grid_step = 0.2
viscosity = 0.1
normal_floor = 0.5


def extended(x, sides, width):
    for axis, dim in sides:
        size, length = (lax.axis_size(axis), x.shape[dim])
        up = [(i, (i + 1) % size) for i in range(size)]
        down = [(j, i) for i, j in up]
        last = lax.slice_in_dim(x, length - width, length, axis=dim)
        leading = lax.slice_in_dim(x, 0, width, axis=dim)
        before = lax.ppermute(last, axis, up)
        after = lax.ppermute(leading, axis, down)
        x = jnp.concatenate([before, x, after], axis=dim)
    return x


def neighbour(values, across, forward):
    length = values.shape[-2]
    plane_size = values.shape[-1]
    if across == 0:
        if forward:
            return jnp.concatenate([values[..., 1:, :], values[..., -1:, :]], axis=-2)
        return jnp.concatenate([values[..., :1, :], values[..., :-1, :]], axis=-2)
    stride = length if across == 1 else 1
    places = jnp.arange(plane_size, dtype=jnp.int32)
    column = places // length if across == 1 else places % length
    if forward:
        shifted = jnp.concatenate([values[..., stride:], values[..., :stride]], axis=-1)
        return jnp.where(column == length - 1, values, shifted)
    shifted = jnp.concatenate(
        [values[..., plane_size - stride :], values[..., : plane_size - stride]], axis=-1
    )
    return jnp.where(column == 0, values, shifted)


def weno_blend(slope_one, slope_two, slope_three, slope_four, slope_five):
    smooth_one = (
        13.0 / 12.0 * (slope_one - 2.0 * slope_two + slope_three) ** 2
        + 0.25 * (slope_one - 4.0 * slope_two + 3.0 * slope_three) ** 2
    )
    smooth_two = (
        13.0 / 12.0 * (slope_two - 2.0 * slope_three + slope_four) ** 2
        + 0.25 * (slope_two - slope_four) ** 2
    )
    smooth_three = (
        13.0 / 12.0 * (slope_three - 2.0 * slope_four + slope_five) ** 2
        + 0.25 * (3.0 * slope_three - 4.0 * slope_four + slope_five) ** 2
    )
    weight_one = 0.1 / (weno_floor + smooth_one) ** 2
    weight_two = 0.6 / (weno_floor + smooth_two) ** 2
    weight_three = 0.3 / (weno_floor + smooth_three) ** 2
    poly_one = slope_one / 3.0 - 7.0 * slope_two / 6.0 + 11.0 * slope_three / 6.0
    poly_two = -slope_two / 6.0 + 5.0 * slope_three / 6.0 + slope_four / 3.0
    poly_three = slope_three / 3.0 + 5.0 * slope_four / 6.0 - slope_five / 6.0
    return (weight_one * poly_one + weight_two * poly_two + weight_three * poly_three) / (
        weight_one + weight_two + weight_three
    )


def upwind_slopes(values, across):
    behind = values - neighbour(values, across, False)
    back_one = neighbour(behind, across, False)
    back_two = neighbour(back_one, across, False)
    ahead_one = neighbour(behind, across, True)
    ahead_two = neighbour(ahead_one, across, True)
    ahead_three = neighbour(ahead_two, across, True)
    minus_side = weno_blend(back_two, back_one, behind, ahead_one, ahead_two)
    plus_side = weno_blend(ahead_three, ahead_two, ahead_one, behind, back_one)
    return (minus_side, plus_side)


def central_slopes(values):
    return [
        0.5 * (neighbour(values, across, True) - neighbour(values, across, False))
        for across in range(3)
    ]


def evolve_boxes(levels, motion):
    change = jnp.zeros_like(levels)
    for across in range(3):
        minus_side, plus_side = upwind_slopes(levels, across)
        speed_d = motion[:, across]
        change = (
            change + jnp.maximum(speed_d, 0.0) * minus_side + jnp.minimum(speed_d, 0.0) * plus_side
        )
    advected = levels - box_step * change
    sign_soft = advected / jnp.sqrt(advected * advected + 1.0)
    outside = advected > 0.0

    def one_sweep(counter, current):
        squared = jnp.zeros_like(current)
        for across in range(3):
            behind = current - neighbour(current, across, False)
            ahead_d = neighbour(current, across, True) - current
            upper_sq = jnp.maximum(jnp.maximum(behind, 0.0) ** 2, jnp.minimum(ahead_d, 0.0) ** 2)
            lower_sq = jnp.maximum(jnp.minimum(behind, 0.0) ** 2, jnp.maximum(ahead_d, 0.0) ** 2)
            squared = squared + jnp.where(outside, upper_sq, lower_sq)
        return current - pseudo_step * sign_soft * (jnp.sqrt(squared) - 1.0)

    settled = lax.fori_loop(0, ITERS, one_sweep, advected)
    slopes = central_slopes(settled)
    magnitude = jnp.maximum(
        jnp.sqrt(slopes[0] ** 2 + slopes[1] ** 2 + slopes[2] ** 2), normal_floor
    )
    bending = jnp.zeros_like(settled)
    for across in range(3):
        unit_d = slopes[across] / magnitude
        bending = bending + 0.5 * (
            neighbour(unit_d, across, True) - neighbour(unit_d, across, False)
        )
    return (settled, bending)


def surface_force(levels, bending):
    slopes = central_slopes(levels)
    delta_band = jnp.exp(-((levels / band_width) ** 2)) / (band_width * math.sqrt(math.pi))
    strength = tension * bending * delta_band
    return jnp.stack([strength * slopes[0], strength * slopes[1], strength * slopes[2]], axis=1)


def tendency(padded):
    centre = padded[:, 1:-1, 1:-1, 1:-1]
    uppers = (padded[:, 2:, 1:-1, 1:-1], padded[:, 1:-1, 2:, 1:-1], padded[:, 1:-1, 1:-1, 2:])
    lowers = (padded[:, :-2, 1:-1, 1:-1], padded[:, 1:-1, :-2, 1:-1], padded[:, 1:-1, 1:-1, :-2])
    advect = jnp.zeros_like(centre)
    spread = -6.0 * centre
    for across in range(3):
        advect = advect + centre[across : across + 1] * (uppers[across] - lowers[across]) * 0.5
        spread = spread + uppers[across] + lowers[across]
    return viscosity * spread - advect


def face_pad(values):
    return extended(values, (("gx", 1), ("gy", 2), ("gz", 3)), 1)


def local(velocity, box_level, corners, owner_list):
    slot_count = box_level.shape[0]
    box_edge = box_level.shape[1]
    alive_mask = (owner_list >= 0).astype(jnp.float32)
    nought = jnp.zeros((), jnp.int32)

    def cut_slot(slot_no, boxes_now):
        corner_at = (nought, corners[slot_no, 0], corners[slot_no, 1], corners[slot_no, 2])
        region = lax.dynamic_slice(velocity, corner_at, (3, box_edge, box_edge, box_edge))
        return boxes_now.at[slot_no].set(region.reshape(3, box_edge, box_edge * box_edge))

    motion_boxes = lax.fori_loop(
        0,
        slot_count,
        cut_slot,
        jnp.zeros((slot_count, 3, box_edge, box_edge * box_edge), jnp.float32),
    )
    settled, bending = evolve_boxes(box_level, motion_boxes)
    settled = settled * alive_mask[:, None, None]
    bending = bending * alive_mask[:, None, None]
    predictor = velocity + grid_step * tendency(face_pad(velocity))
    second = predictor + grid_step * tendency(face_pad(predictor))
    stepped = 0.5 * (velocity + second)
    push_boxes = surface_force(settled, bending).reshape(
        slot_count, 3, box_edge, box_edge, box_edge
    )

    def deposit_slot(slot_no, grid_now):
        corner_at = (nought, corners[slot_no, 0], corners[slot_no, 1], corners[slot_no, 2])
        region = lax.dynamic_slice(grid_now, corner_at, (3, box_edge, box_edge, box_edge))
        return lax.dynamic_update_slice(
            grid_now, region + grid_step * push_boxes[slot_no], corner_at
        )

    result = lax.fori_loop(0, slot_count, deposit_slot, stepped)
    return (result, settled, bending)


def solution(mesh):
    placed = (
        P(None, "gx", "gy", "gz"),
        P(("gx", "gy", "gz"), None, None),
        P(("gx", "gy", "gz"), None),
        P(("gx", "gy", "gz")),
    )
    return jax.shard_map(
        local,
        mesh=mesh,
        in_specs=placed,
        out_specs=(
            P(None, "gx", "gy", "gz"),
            P(("gx", "gy", "gz"), None, None),
            P(("gx", "gy", "gz"), None, None),
        ),
        check_vma=False,
    )
```

profile of v0, /device:TPU:0, one launch (start us, length us, event | category | flops | bytes accessed | tf_op | source)
XLA Modules:
  0.0 749.7 jit_solution(4137843093980891951)
XLA Ops:
  15.2 174.6 %while.39 = (s32[]{:T(128)}, f32[16,3,16,256]{3,2,0,1:T(8,128)}, s32[16,3]{0,1:T(4,128)}, f32[3,32,32,128]{3,2,1,0:T(8,128)S(1)}, s32[]{:T(128)}, /*index=5*/s32...) while((s32[]{:T(128)}, f32[16,3,16,256]{3,2,0,1:T(8,128)}, s32[16,3]{0,1:T(4,128)}, ...), condition=%wide.region_2.0_spmd, body=%wide.region_0.0_spmd.sunk | while | flops 12326 | bytes 443672 | solution.py:166
  192.3 5.4 broadcast_compare_fusion.4
  197.8 15.8 %while.40 = (s32[]{:T(128)}, f32[16,16,256]{2,1,0:T(8,128)S(1)}, f32[16,16,256]{2,1,0:T(8,128)S(1)}, pred[16,16,256]{2,1,0:T(8,128)(4,1)S(1)}, s32[]{:T(128)}) while((s32[]{:T(128)}, f32[16,16,256]{2,1,0:T(8,128)S(1)}, f32[16,16,256]{2,1,0:T(8,128)S(1)}, pred[16,16,256]{2,1,0:T(8,128)(4,1)S(1)}, s32[]{:T(128)}) %tuple.168), condition=%wide.region_4.5_spmd, body=%wide.region_3.4_spmd.sunk | while | flops 3611650 | bytes 5572669 | solution.py:118
  242.2 6.8 multiply_add_fusion
  262.1 6.2 pad_maximum_fusion
  277.4 3.6 collective-permute-start.10
  286.7 7.3 add_multiply_fusion
  293.9 455.6 %while.41 = (s32[]{:T(128)}, f32[3,32,32,128]{3,2,1,0:T(8,128)}, s32[16,3]{0,1:T(4,128)}, f32[16,3,16,16,16]{4,3,2,1,0:T(8,128)}, s32[]{:T(128)}, /*index=5*/s32[]{:T(128)}, s32[]{:T(128)}, s32[]{:T(128)}) while((s32[]{:T(128)}, f32[3,32,32,128]{3,2,1,0:T(8,128)}, s32[16,3]{0,1:T(4,128)}, f32[16,3,16,16,16]{4,3,2,1,0:T(8,128)}, s32[]{:T(128)}, ...), condition=%wide.region_6.7_spmd, body=%wide.region_5.6_spmd.sunk | while | flops 24587 | bytes 246003 | solution.py:189
  302.4 20.0 %dynamic_update_slice.8 = f32[3,32,32,128]{3,2,1,0:T(8,128)} dynamic-update-slice(f32[3,32,32,128]{3,2,1,0:T(8,128)} %get-tuple-element.555, f32[3,16,16,16]{3,2,1,0:T(8,128)S(1)} %bitcast_add_fusion.2, s32[]{:T(128)} %constant.370.clone.1..sunk.1, s32[]{:T(128)S(6)} %select_n.460, s32[]{:T(128)S(6)} %select_n.461, s32[]{:T(128)S(6)} %select_n.462) | dynamic-update-slice | bytes 98308 | tf_op jit(solution)/shard_map/while/body/eval_jaxpr/dynamic_update_slice | solution.py:185
  330.9 20.0 %dynamic_update_slice.8 = f32[3,32,32,128]{3,2,1,0:T(8,128)} dynamic-update-slice(f32[3,32,32,128]{3,2,1,0:T(8,128)} %get-tuple-element.555, f32[3,16,16,16]{3,2,1,0:T(8,128)S(1)} %bitcast_add_fusion.2, s32[]{:T(128)} %constant.370.clone.1..sunk.1, s32[]{:T(128)S(6)} %select_n.460, s32[]{:T(128)S(6)} %select_n.461, s32[]{:T(128)S(6)} %select_n.462) | dynamic-update-slice | bytes 98308 | tf_op jit(solution)/shard_map/while/body/eval_jaxpr/dynamic_update_slice | solution.py:185
  359.4 20.0 %dynamic_update_slice.8 = f32[3,32,32,128]{3,2,1,0:T(8,128)} dynamic-update-slice(f32[3,32,32,128]{3,2,1,0:T(8,128)} %get-tuple-element.555, f32[3,16,16,16]{3,2,1,0:T(8,128)S(1)} %bitcast_add_fusion.2, s32[]{:T(128)} %constant.370.clone.1..sunk.1, s32[]{:T(128)S(6)} %select_n.460, s32[]{:T(128)S(6)} %select_n.461, s32[]{:T(128)S(6)} %select_n.462) | dynamic-update-slice | bytes 98308 | tf_op jit(solution)/shard_map/while/body/eval_jaxpr/dynamic_update_slice | solution.py:185
  387.8 20.0 %dynamic_update_slice.8 = f32[3,32,32,128]{3,2,1,0:T(8,128)} dynamic-update-slice(f32[3,32,32,128]{3,2,1,0:T(8,128)} %get-tuple-element.555, f32[3,16,16,16]{3,2,1,0:T(8,128)S(1)} %bitcast_add_fusion.2, s32[]{:T(128)} %constant.370.clone.1..sunk.1, s32[]{:T(128)S(6)} %select_n.460, s32[]{:T(128)S(6)} %select_n.461, s32[]{:T(128)S(6)} %select_n.462) | dynamic-update-slice | bytes 98308 | tf_op jit(solution)/shard_map/while/body/eval_jaxpr/dynamic_update_slice | solution.py:185
  416.3 20.0 %dynamic_update_slice.8 = f32[3,32,32,128]{3,2,1,0:T(8,128)} dynamic-update-slice(f32[3,32,32,128]{3,2,1,0:T(8,128)} %get-tuple-element.555, f32[3,16,16,16]{3,2,1,0:T(8,128)S(1)} %bitcast_add_fusion.2, s32[]{:T(128)} %constant.370.clone.1..sunk.1, s32[]{:T(128)S(6)} %select_n.460, s32[]{:T(128)S(6)} %select_n.461, s32[]{:T(128)S(6)} %select_n.462) | dynamic-update-slice | bytes 98308 | tf_op jit(solution)/shard_map/while/body/eval_jaxpr/dynamic_update_slice | solution.py:185
  444.8 20.0 %dynamic_update_slice.8 = f32[3,32,32,128]{3,2,1,0:T(8,128)} dynamic-update-slice(f32[3,32,32,128]{3,2,1,0:T(8,128)} %get-tuple-element.555, f32[3,16,16,16]{3,2,1,0:T(8,128)S(1)} %bitcast_add_fusion.2, s32[]{:T(128)} %constant.370.clone.1..sunk.1, s32[]{:T(128)S(6)} %select_n.460, s32[]{:T(128)S(6)} %select_n.461, s32[]{:T(128)S(6)} %select_n.462) | dynamic-update-slice | bytes 98308 | tf_op jit(solution)/shard_map/while/body/eval_jaxpr/dynamic_update_slice | solution.py:185
  473.2 20.0 %dynamic_update_slice.8 = f32[3,32,32,128]{3,2,1,0:T(8,128)} dynamic-update-slice(f32[3,32,32,128]{3,2,1,0:T(8,128)} %get-tuple-element.555, f32[3,16,16,16]{3,2,1,0:T(8,128)S(1)} %bitcast_add_fusion.2, s32[]{:T(128)} %constant.370.clone.1..sunk.1, s32[]{:T(128)S(6)} %select_n.460, s32[]{:T(128)S(6)} %select_n.461, s32[]{:T(128)S(6)} %select_n.462) | dynamic-update-slice | bytes 98308 | tf_op jit(solution)/shard_map/while/body/eval_jaxpr/dynamic_update_slice | solution.py:185
  501.7 20.0 %dynamic_update_slice.8 = f32[3,32,32,128]{3,2,1,0:T(8,128)} dynamic-update-slice(f32[3,32,32,128]{3,2,1,0:T(8,128)} %get-tuple-element.555, f32[3,16,16,16]{3,2,1,0:T(8,128)S(1)} %bitcast_add_fusion.2, s32[]{:T(128)} %constant.370.clone.1..sunk.1, s32[]{:T(128)S(6)} %select_n.460, s32[]{:T(128)S(6)} %select_n.461, s32[]{:T(128)S(6)} %select_n.462) | dynamic-update-slice | bytes 98308 | tf_op jit(solution)/shard_map/while/body/eval_jaxpr/dynamic_update_slice | solution.py:185
  530.2 20.0 %dynamic_update_slice.8 = f32[3,32,32,128]{3,2,1,0:T(8,128)} dynamic-update-slice(f32[3,32,32,128]{3,2,1,0:T(8,128)} %get-tuple-element.555, f32[3,16,16,16]{3,2,1,0:T(8,128)S(1)} %bitcast_add_fusion.2, s32[]{:T(128)} %constant.370.clone.1..sunk.1, s32[]{:T(128)S(6)} %select_n.460, s32[]{:T(128)S(6)} %select_n.461, s32[]{:T(128)S(6)} %select_n.462) | dynamic-update-slice | bytes 98308 | tf_op jit(solution)/shard_map/while/body/eval_jaxpr/dynamic_update_slice | solution.py:185
  558.7 20.0 %dynamic_update_slice.8 = f32[3,32,32,128]{3,2,1,0:T(8,128)} dynamic-update-slice(f32[3,32,32,128]{3,2,1,0:T(8,128)} %get-tuple-element.555, f32[3,16,16,16]{3,2,1,0:T(8,128)S(1)} %bitcast_add_fusion.2, s32[]{:T(128)} %constant.370.clone.1..sunk.1, s32[]{:T(128)S(6)} %select_n.460, s32[]{:T(128)S(6)} %select_n.461, s32[]{:T(128)S(6)} %select_n.462) | dynamic-update-slice | bytes 98308 | tf_op jit(solution)/shard_map/while/body/eval_jaxpr/dynamic_update_slice | solution.py:185
  587.1 20.0 %dynamic_update_slice.8 = f32[3,32,32,128]{3,2,1,0:T(8,128)} dynamic-update-slice(f32[3,32,32,128]{3,2,1,0:T(8,128)} %get-tuple-element.555, f32[3,16,16,16]{3,2,1,0:T(8,128)S(1)} %bitcast_add_fusion.2, s32[]{:T(128)} %constant.370.clone.1..sunk.1, s32[]{:T(128)S(6)} %select_n.460, s32[]{:T(128)S(6)} %select_n.461, s32[]{:T(128)S(6)} %select_n.462) | dynamic-update-slice | bytes 98308 | tf_op jit(solution)/shard_map/while/body/eval_jaxpr/dynamic_update_slice | solution.py:185
  615.6 20.0 %dynamic_update_slice.8 = f32[3,32,32,128]{3,2,1,0:T(8,128)} dynamic-update-slice(f32[3,32,32,128]{3,2,1,0:T(8,128)} %get-tuple-element.555, f32[3,16,16,16]{3,2,1,0:T(8,128)S(1)} %bitcast_add_fusion.2, s32[]{:T(128)} %constant.370.clone.1..sunk.1, s32[]{:T(128)S(6)} %select_n.460, s32[]{:T(128)S(6)} %select_n.461, s32[]{:T(128)S(6)} %select_n.462) | dynamic-update-slice | bytes 98308 | tf_op jit(solution)/shard_map/while/body/eval_jaxpr/dynamic_update_slice | solution.py:185
  644.1 20.0 %dynamic_update_slice.8 = f32[3,32,32,128]{3,2,1,0:T(8,128)} dynamic-update-slice(f32[3,32,32,128]{3,2,1,0:T(8,128)} %get-tuple-element.555, f32[3,16,16,16]{3,2,1,0:T(8,128)S(1)} %bitcast_add_fusion.2, s32[]{:T(128)} %constant.370.clone.1..sunk.1, s32[]{:T(128)S(6)} %select_n.460, s32[]{:T(128)S(6)} %select_n.461, s32[]{:T(128)S(6)} %select_n.462) | dynamic-update-slice | bytes 98308 | tf_op jit(solution)/shard_map/while/body/eval_jaxpr/dynamic_update_slice | solution.py:185
  672.6 20.0 %dynamic_update_slice.8 = f32[3,32,32,128]{3,2,1,0:T(8,128)} dynamic-update-slice(f32[3,32,32,128]{3,2,1,0:T(8,128)} %get-tuple-element.555, f32[3,16,16,16]{3,2,1,0:T(8,128)S(1)} %bitcast_add_fusion.2, s32[]{:T(128)} %constant.370.clone.1..sunk.1, s32[]{:T(128)S(6)} %select_n.460, s32[]{:T(128)S(6)} %select_n.461, s32[]{:T(128)S(6)} %select_n.462) | dynamic-update-slice | bytes 98308 | tf_op jit(solution)/shard_map/while/body/eval_jaxpr/dynamic_update_slice | solution.py:185
  701.0 20.0 %dynamic_update_slice.8 = f32[3,32,32,128]{3,2,1,0:T(8,128)} dynamic-update-slice(f32[3,32,32,128]{3,2,1,0:T(8,128)} %get-tuple-element.555, f32[3,16,16,16]{3,2,1,0:T(8,128)S(1)} %bitcast_add_fusion.2, s32[]{:T(128)} %constant.370.clone.1..sunk.1, s32[]{:T(128)S(6)} %select_n.460, s32[]{:T(128)S(6)} %select_n.461, s32[]{:T(128)S(6)} %select_n.462) | dynamic-update-slice | bytes 98308 | tf_op jit(solution)/shard_map/while/body/eval_jaxpr/dynamic_update_slice | solution.py:185
  729.5 20.0 %dynamic_update_slice.8 = f32[3,32,32,128]{3,2,1,0:T(8,128)} dynamic-update-slice(f32[3,32,32,128]{3,2,1,0:T(8,128)} %get-tuple-element.555, f32[3,16,16,16]{3,2,1,0:T(8,128)S(1)} %bitcast_add_fusion.2, s32[]{:T(128)} %constant.370.clone.1..sunk.1, s32[]{:T(128)S(6)} %select_n.460, s32[]{:T(128)S(6)} %select_n.461, s32[]{:T(128)S(6)} %select_n.462) | dynamic-update-slice | bytes 98308 | tf_op jit(solution)/shard_map/while/body/eval_jaxpr/dynamic_update_slice | solution.py:185
  (412 shorter events, 217.8 us)
Async XLA Ops:
  2.1 216.5 %collective-permute-start.1 = (f32[3,1,32,128]{3,2,1,0:T(8,128)}, f32[3,1,32,128]{3,2,1,0:T(8,128)}, u32[]{:S(2)}, u32[]{:S(2)}) collective-permute-start(f32[3,1,32,128]{3,2,1,0:T(8,128)} %get-tuple-element.317), channel_id=1, source_target_pairs={{0,16},{16,0},{1,17},{17,1},{2,18},{18,2},{3,19},{19,3},{4,20},{20... | collective-permute-start | bytes 147464 | tf_op jit(solution)/shard_map/ppermute | solution.py:28
  5.1 214.4 %collective-permute-start = (f32[3,1,32,128]{3,2,1,0:T(8,128)}, f32[3,1,32,128]{3,2,1,0:T(8,128)}, u32[]{:S(2)}, u32[]{:S(2)}) collective-permute-start(f32[3,1,32,128]{3,2,1,0:T(8,128)} %get-tuple-element.316), channel_id=1, source_target_pairs={{16,0},{0,16},{17,1},{1,17},{18,2},{2,18},{19,3},{3,19},{20,4},{4,... | collective-permute-start | bytes 147464 | tf_op jit(solution)/shard_map/ppermute | solution.py:29
  15.2 175.8 %copy-start.22 = (f32[16,1,256]{2,1,0:T(1,128)S(1)}, f32[16,1,256]{2,1,0:T(1,128)}, u32[]{:S(2)}) copy-start(f32[16,1,256]{2,1,0:T(1,128)} %get-tuple-element.359) | copy-start | bytes 49156
  15.2 177.0 %copy-start.18 = (f32[16,16,1]{2,1,0:T(8,128)S(1)}, f32[16,16,1]{2,1,0:T(8,128)}, u32[]{:S(2)}) copy-start(f32[16,16,1]{2,1,0:T(8,128)} %slice.569) | copy-start | bytes 3076
  214.7 22.2 %copy-start.1 = (f32[16,16,256]{2,1,0:T(8,128)}, f32[16,16,256]{2,1,0:T(8,128)S(1)}, u32[]{:S(2)}) copy-start(f32[16,16,256]{2,1,0:T(8,128)S(1)} %get-tuple-element.338) | copy-start | bytes 786436
  220.4 2.6 collective-permute-start.2
  221.2 3.8 collective-permute-start.3
  230.4 7.2 collective-permute-start.5
  234.5 5.4 collective-permute-start.4
  242.1 9.6 %copy-start.2 = (f32[16,16,256]{2,1,0:T(8,128)S(1)}, f32[16,16,256]{2,1,0:T(8,128)}, u32[]{:S(2)}) copy-start(f32[16,16,256]{2,1,0:T(8,128)} %copy-done.1) | copy-start | bytes 786436
  242.1 9.6 %copy-start.13 = (f32[16,16,240]{2,1,0:T(8,128)S(1)}, f32[16,16,240]{2,1,0:T(8,128)}, u32[]{:S(2)}) copy-start(f32[16,16,240]{2,1,0:T(8,128)} %get-tuple-element.322) | copy-start | bytes 737284
  242.1 9.6 %copy-start.14 = (f32[16,16,240]{2,1,0:T(8,128)S(1)}, f32[16,16,240]{2,1,0:T(8,128)}, u32[]{:S(2)}) copy-start(f32[16,16,240]{2,1,0:T(8,128)} %get-tuple-element.323) | copy-start | bytes 737284
  242.1 9.6 %copy-start.15 = (f32[16,16,255]{2,1,0:T(8,128)S(1)}, f32[16,16,255]{2,1,0:T(8,128)}, u32[]{:S(2)}) copy-start(f32[16,16,255]{2,1,0:T(8,128)} %get-tuple-element.357) | copy-start | bytes 783364
  242.1 9.6 %copy-start.16 = (f32[16,16,255]{2,1,0:T(8,128)S(1)}, f32[16,16,255]{2,1,0:T(8,128)}, u32[]{:S(2)}) copy-start(f32[16,16,255]{2,1,0:T(8,128)} %get-tuple-element.358) | copy-start | bytes 783364
  242.1 9.6 %copy-start.17 = (f32[16,16,256]{2,1,0:T(8,128)S(1)}, f32[16,16,256]{2,1,0:T(8,128)}, u32[]{:S(2)}) copy-start(f32[16,16,256]{2,1,0:T(8,128)} %get-tuple-element.272) | copy-start | bytes 786436
  242.2 9.6 %copy-start.19 = (f32[16,16,16]{2,1,0:T(8,128)S(1)}, f32[16,16,16]{2,1,0:T(8,128)}, u32[]{:S(2)}) copy-start(f32[16,16,16]{2,1,0:T(8,128)} %get-tuple-element.321) | copy-start | bytes 49156
  242.2 9.6 %copy-start.20 = (f32[16,16,1]{2,1,0:T(8,128)S(1)}, f32[16,16,1]{2,1,0:T(8,128)}, u32[]{:S(2)}) copy-start(f32[16,16,1]{2,1,0:T(8,128)} %get-tuple-element.355) | copy-start | bytes 3076
  242.2 9.6 %copy-start.21 = (f32[16,16,1]{2,1,0:T(8,128)S(1)}, f32[16,16,1]{2,1,0:T(8,128)}, u32[]{:S(2)}) copy-start(f32[16,16,1]{2,1,0:T(8,128)} %get-tuple-element.356) | copy-start | bytes 3076
  249.7 11.0 %collective-permute-start.6 = (f32[3,1,32,128]{3,2,1,0:T(8,128)}, f32[3,1,32,128]{3,2,1,0:T(8,128)}, u32[]{:S(2)}, u32[]{:S(2)}) collective-permute-start(f32[3,1,32,128]{3,2,1,0:T(8,128)} %get-tuple-element.312), channel_id=1, source_target_pairs={{16,0},{0,16},{17,1},{1,17},{18,2},{2,18},{19,3},{3,19},{20,4},{4,... | collective-permute-start | bytes 147464 | tf_op jit(solution)/shard_map/ppermute | solution.py:29
  251.2 9.4 %collective-permute-start.7 = (f32[3,1,32,128]{3,2,1,0:T(8,128)}, f32[3,1,32,128]{3,2,1,0:T(8,128)}, u32[]{:S(2)}, u32[]{:S(2)}) collective-permute-start(f32[3,1,32,128]{3,2,1,0:T(8,128)} %get-tuple-element.311), channel_id=1, source_target_pairs={{0,16},{16,0},{1,17},{17,1},{2,18},{18,2},{3,19},{19,3},{4,20},{20... | collective-permute-start | bytes 147464 | tf_op jit(solution)/shard_map/ppermute | solution.py:28
  261.5 6.8 collective-permute-start.8
  261.6 6.7 collective-permute-start.9
  274.5 7.8 %collective-permute-start.11 = (f32[3,34,34,1]{2,3,1,0:T(1,128)S(1)}, f32[3,34,34,1]{2,3,1,0:T(1,128)S(1)}, u32[]{:S(2)}, u32[]{:S(2)}) collective-permute-start(f32[3,34,34,1]{2,3,1,0:T(1,128)S(1)} %copy.77), channel_id=1, source_target_pairs={{0,1},{1,2},{2,3},{3,0},{4,5},{5,6},{6,7},{7,4},{8,9},{9,10},{10,1... | collective-permute-start | bytes 41624 | tf_op jit(solution)/shard_map/ppermute | solution.py:28
  277.4 7.1 collective-permute-start.10
  (26 other events, 91.4 us)
where the time goes:
time: 755 us; the launch traced here: 750 us
  local copies, waits for them, and re-layouts  442 us (59%)
  loops' own time  181 us (24%)
  other arithmetic  107 us (14%)
  starting transfers between devices  14.7 us (2%)
    dynamic_update_slice x16, local copies, waits for them, and re-layouts, deposit_slot(): lax.dynamic_update_slice(grid_now, region + grid_step * push_boxes[slot_n...  320 us
    another operation x1, loops' own time, local(): result = lax.fori_loop(0, slot_count, deposit_slot, stepped)  90.3 us
    another operation x1, loops' own time, local(): lax.fori_loop(0, slot_count, cut_slot, jnp.zeros((slot_count, 3, box_edge...  89.9 us
    dynamic_slice x16, local copies, waits for them, and re-layouts, deposit_slot(): corners[slot_no, 2]  23.3 us
    dynamic_slice x16, local copies, waits for them, and re-layouts, cut_slot(): corners[slot_no, 2]  23.2 us
    another operation x16, other arithmetic  22.8 us
    add x16, other arithmetic, deposit_slot(): region + grid_step * push_boxes[slot_no]  22 us
    scatter x16, other arithmetic, cut_slot(): boxes_now.at[slot_no].set(region.reshape(3, box_edge, box_edge * box_edge))  19.9 us
  transfers between devices with their start and end apart: 12, of which 2 were waited for; matrix products, arithmetic and copies ran while one was open for 20% of the time, Pallas kernels for 0%

commit v1 on v0

v1 whole, which is shorter than its diff:
```python
import functools
import math

import jax
import jax.numpy as jnp
from jax import lax
from jax.experimental import pallas as pl
from jax.experimental.pallas import tpu as pltpu
from jax.sharding import PartitionSpec as P

ITERS = 12

box_step = 0.25
pseudo_step = 0.3
weno_floor = 1e-06
band_width = 1.5
tension = 2.0
grid_step = 0.2
viscosity = 0.1
normal_floor = 0.5
tiny = 1.1754944e-38

MESH = pl.DeviceIdType.MESH


def iota(shape, dim):
    return lax.broadcasted_iota(jnp.int32, shape, dim)


def pack_z(ext, dst, xs, ys, lanes):
    group = iota((ys, lanes), 1) // 4

    def step(x, accs):
        shift = 4 * x + 1
        return tuple(
            jnp.where(group == x, pltpu.roll(ext[c, x + 1], shift, 1), accs[c]) for c in range(3)
        )

    accs = lax.fori_loop(
        0, xs, step, tuple(jnp.zeros((ys, lanes), jnp.float32) for _ in range(3)), unroll=4
    )
    for c in range(3):
        dst[c] = accs[c]


def momentum_kernel(
    sizes, v_hbm, o_ref, ext1, ext2, ysend, yrecv, zsend, zrecv, comb, local_sem, send_sem, recv_sem
):
    _, xs, ys, lanes = v_hbm.shape
    load = pltpu.make_async_copy(v_hbm, ext1.at[:, pl.ds(1, xs)], local_sem)
    load.start()
    ups, downs = [], []
    for axis in ("gx", "gy", "gz"):
        me, n = lax.axis_index(axis), sizes[axis]
        ups.append({axis: lax.rem(me + 1, n)})
        downs.append({axis: lax.rem(me + n - 1, n)})
    barrier = pltpu.get_barrier_semaphore()
    for target in ups + downs:
        pl.semaphore_signal(barrier, inc=1, device_id=target, device_id_type=MESH)
    pl.semaphore_wait(barrier, 6)
    load.wait()

    def exchange(r, ext):
        copies = []

        def send(n, src, dst, target):
            copy = pltpu.make_async_remote_copy(
                src_ref=src,
                dst_ref=dst,
                send_sem=send_sem.at[r, n],
                recv_sem=recv_sem.at[r, n],
                device_id=target,
                device_id_type=MESH,
            )
            copy.start()
            copies.append(copy)

        for c in range(3):
            ysend[r, 0, c] = ext[c, pl.ds(1, xs), ys - 1, :]
            ysend[r, 1, c] = ext[c, pl.ds(1, xs), 0, :]
        pack_z(ext, zsend.at[r], xs, ys, lanes)
        send(0, ext.at[:, xs], ext.at[:, 0], ups[0])
        send(1, ext.at[:, 1], ext.at[:, xs + 1], downs[0])
        send(2, ysend.at[r, 0], yrecv.at[r, 0], ups[1])
        send(3, ysend.at[r, 1], yrecv.at[r, 1], downs[1])
        send(4, zsend.at[r], zrecv.at[r, 0], ups[2])
        send(5, zsend.at[r], zrecv.at[r, 1], downs[2])
        return copies

    lane = iota((ys, lanes), 1)
    row = iota((ys, lanes), 0)
    quarter = lane % 4

    def section(r, ext, emit):
        for c in range(3):
            comb[c] = jnp.where(
                quarter == 0,
                pltpu.roll(zrecv[r, 1, c], lanes - 1, 1),
                pltpu.roll(zrecv[r, 0, c], 1, 1),
            )

        def step(x, carry):
            centre = [ext[c, x + 1] for c in range(3)]
            for c in range(3):
                mid = centre[c]
                x_lo, x_hi = ext[c, x], ext[c, x + 2]
                y_lo = jnp.where(row == 0, yrecv[r, 0, c, pl.ds(x, 1), :], pltpu.roll(mid, 1, 0))
                y_hi = jnp.where(
                    row == ys - 1, yrecv[r, 1, c, pl.ds(x, 1), :], pltpu.roll(mid, ys - 1, 0)
                )
                halo = pltpu.roll(comb[c], lanes - 1 - 4 * x, 1)
                z_lo = jnp.where(lane == 0, halo, pltpu.roll(mid, 1, 1))
                z_hi = jnp.where(lane == lanes - 1, halo, pltpu.roll(mid, lanes - 1, 1))
                spread = (x_hi + x_lo) + (y_hi + y_lo) + (z_hi + z_lo) - 6.0 * mid
                advect = (
                    centre[0] * (x_hi - x_lo) + centre[1] * (y_hi - y_lo) + centre[2] * (z_hi - z_lo)
                )
                emit(c, x, mid + grid_step * (viscosity * spread - 0.5 * advect))
            return carry

        lax.fori_loop(0, xs, step, 0)

    def first(c, x, value):
        ext2[c, x + 1] = value

    def second(c, x, value):
        o_ref[c, x] = 0.5 * (ext1[c, x + 1] + value)

    for copy in exchange(0, ext1):
        copy.wait()
    section(0, ext1, first)
    for copy in exchange(1, ext2):
        copy.wait()
    section(1, ext2, second)


def momentum(velocity):
    sizes = {axis: lax.axis_size(axis) for axis in ("gx", "gy", "gz")}
    _, xs, ys, lanes = velocity.shape
    vmem = pltpu.VMEM
    f32 = jnp.float32
    return pl.pallas_call(
        functools.partial(momentum_kernel, sizes),
        out_shape=jax.ShapeDtypeStruct(velocity.shape, f32),
        in_specs=[pl.BlockSpec(memory_space=pl.ANY)],
        out_specs=pl.BlockSpec(memory_space=pltpu.VMEM),
        scratch_shapes=[
            vmem((3, xs + 2, ys, lanes), f32),
            vmem((3, xs + 2, ys, lanes), f32),
            vmem((2, 2, 3, xs, lanes), f32),
            vmem((2, 2, 3, xs, lanes), f32),
            vmem((2, 3, ys, lanes), f32),
            vmem((2, 2, 3, ys, lanes), f32),
            vmem((3, ys, lanes), f32),
            pltpu.SemaphoreType.DMA(()),
            pltpu.SemaphoreType.DMA((2, 6)),
            pltpu.SemaphoreType.DMA((2, 6)),
        ],
        compiler_params=pltpu.CompilerParams(collective_id=0, has_side_effects=True),
    )(velocity)


def blend(a, b, c, e, f):
    s1 = 13.0 / 12.0 * (a - 2.0 * b + c) ** 2 + 0.25 * (a - 4.0 * b + 3.0 * c) ** 2
    s2 = 13.0 / 12.0 * (b - 2.0 * c + e) ** 2 + 0.25 * (b - e) ** 2
    s3 = 13.0 / 12.0 * (c - 2.0 * e + f) ** 2 + 0.25 * (3.0 * c - 4.0 * e + f) ** 2
    a1, a2, a3 = [(weno_floor + s) ** 2 for s in (s1, s2, s3)]
    n1, n2, n3 = 0.1 * (a2 * a3), 0.6 * (a1 * a3), 0.3 * (a1 * a2)
    p1 = a * (1.0 / 3.0) - b * (7.0 / 6.0) + c * (11.0 / 6.0)
    p2 = b * (-1.0 / 6.0) + c * (5.0 / 6.0) + e * (1.0 / 3.0)
    p3 = c * (1.0 / 3.0) + e * (5.0 / 6.0) - f * (1.0 / 6.0)
    return (n1 * p1 + n2 * p2 + n3 * p3) / (n1 + n2 + n3)


def bubble_kernel(
    corners, owners, v_ref, lev_ref, step_ref, o_ref, set_ref, ben_ref,
    lev, mot, psa, psb, gain, force, part, nrm, native_a, native_b,
):
    edge = lev.shape[0]
    rows, lanes = lev.shape[1:]
    groups = rows // edge
    per = lanes // edge
    halves = edge // 8
    row, lane = iota((rows, lanes), 0), iota((rows, lanes), 1)
    j_at, k_at = row % edge, lane % edge
    j_first, j_last = j_at == 0, j_at == edge - 1
    k_first, k_last = k_at == 0, k_at == edge - 1

    def prev_j(x):
        return jnp.where(j_first, x, pltpu.roll(x, 1, 0))

    def next_j(x):
        return jnp.where(j_last, x, pltpu.roll(x, rows - 1, 0))

    def prev_k(x):
        return jnp.where(k_first, x, pltpu.roll(x, 1, 1))

    def next_k(x):
        return jnp.where(k_last, x, pltpu.roll(x, lanes - 1, 1))

    def swap_blocks(x):
        block = lane // edge
        for b in (1, 2, 4):
            low = jnp.logical_and((row & b) != 0, (block & b) == 0)
            high = jnp.logical_and((row & b) == 0, (block & b) != 0)
            down = pltpu.roll(pltpu.roll(x, b, 0), lanes - edge * b, 1)
            up = pltpu.roll(pltpu.roll(x, rows - b, 0), edge * b, 1)
            x = jnp.where(low, down, jnp.where(high, up, x))
        return x

    for h in range(halves):
        native_a[h] = lev_ref[:, pl.ds(h * lanes, lanes)]

    def fetch(i, carry):
        pieces = [
            native_a[h, pl.ds(g * per * edge + i, per, stride=edge), :]
            for g in range(groups)
            for h in range(halves)
        ]
        lev[i] = swap_blocks(jnp.concatenate(pieces, axis=0))
        return carry

    lax.fori_loop(0, edge, fetch, 0)

    def write(ref, i, value):
        value = swap_blocks(value)
        for g in range(groups):
            for h in range(halves):
                at = g * edge + h * 8
                ref[h, pl.ds(g * per * edge + i, per, stride=edge), :] = value[at : at + 8]

    slot_lane = iota((edge, lanes), 1) // edge
    for g in range(groups):
        places = [[corners[g * per + s, d] for d in range(3)] for s in range(per)]
        turns = [lax.rem(s * edge + lanes - places[s][2], lanes) for s in range(per)]

        def gather(i, carry, g=g, places=places, turns=turns):
            for c in range(3):
                acc = jnp.zeros((edge, lanes), jnp.float32)
                for s in range(per):
                    block = v_ref[c, places[s][0] + i, pl.ds(places[s][1], edge), :]
                    acc = jnp.where(slot_lane == s, pltpu.roll(block, turns[s], 1), acc)
                mot[c, i, pl.ds(g * edge, edge), :] = acc
            return carry

        lax.fori_loop(0, edge, gather, 0)

    def advect(i, carry):
        here = lev[i]
        change = jnp.zeros_like(here)
        for d in range(3):
            if d == 0:
                slopes = []
                for t in range(-2, 4):
                    at = jnp.clip(i + t, 0, edge - 1)
                    slopes.append(lev[at] - lev[jnp.maximum(at - 1, 0)])
            else:
                back, ahead = (prev_j, next_j) if d == 1 else (prev_k, next_k)
                mid = here - back(here)
                b1 = back(mid)
                f1 = ahead(mid)
                f2 = ahead(f1)
                slopes = [back(b1), b1, mid, f1, f2, ahead(f2)]
            speed = mot[d, i]
            pos = speed > 0.0
            picks = [jnp.where(pos, slopes[n], slopes[5 - n]) for n in range(5)]
            change = change + speed * blend(*picks)
        out = here - box_step * change
        psa[i] = out
        gain[i] = pseudo_step * out * lax.rsqrt(out * out + 1.0)
        return carry

    lax.fori_loop(0, edge, advect, 0)

    def sweep(src, dst):
        for i in range(edge):
            cur = src[i]
            rate = gain[i]
            sign = jnp.where(rate > 0.0, 1.0, -1.0)
            signed = sign * cur
            total = None
            for lo, hi in (
                (src[max(i - 1, 0)], src[min(i + 1, edge - 1)]),
                (prev_j(cur), next_j(cur)),
                (prev_k(cur), next_k(cur)),
            ):
                rise = jnp.maximum(signed - jnp.minimum(sign * lo, sign * hi), 0.0)
                total = rise * rise if total is None else total + rise * rise
            root = total * lax.rsqrt(jnp.maximum(total, tiny))
            dst[i] = cur - rate * (root - 1.0)

    def two_sweeps(n, carry):
        sweep(psa, psb)
        sweep(psb, psa)
        return carry

    lax.fori_loop(0, ITERS // 2, two_sweeps, 0)

    alive = jnp.zeros((rows, lanes), jnp.float32)
    owner_at = (row // edge) * per + lane // edge
    for s in range(groups * per):
        alive = jnp.where(owner_at == s, jnp.where(owners[s] >= 0, 1.0, 0.0), alive)

    def bend(i, carry):
        cur = psa[i]
        c0 = 0.5 * (psa[jnp.minimum(i + 1, edge - 1)] - psa[jnp.maximum(i - 1, 0)])
        c1 = 0.5 * (next_j(cur) - prev_j(cur))
        c2 = 0.5 * (next_k(cur) - prev_k(cur))
        inverse = lax.rsqrt(jnp.maximum(c0 * c0 + c1 * c1 + c2 * c2, normal_floor * normal_floor))
        n1, n2 = c1 * inverse, c2 * inverse
        nrm[i] = c0 * inverse
        part[i] = 0.5 * (next_j(n1) - prev_j(n1)) + 0.5 * (next_k(n2) - prev_k(n2))
        force[0, i] = c0
        force[1, i] = c1
        force[2, i] = c2
        return carry

    lax.fori_loop(0, edge, bend, 0)

    def push(i, carry):
        level = psa[i] * alive
        curve = (
            part[i] + 0.5 * (nrm[jnp.minimum(i + 1, edge - 1)] - nrm[jnp.maximum(i - 1, 0)])
        ) * alive
        write(native_a, i, level)
        write(native_b, i, curve)
        ratio = level * (1.0 / band_width)
        scale = grid_step * tension / (band_width * math.sqrt(math.pi))
        strength = scale * curve * jnp.exp(-(ratio * ratio)) * alive
        for d in range(3):
            force[d, i] = force[d, i] * strength
        return carry

    lax.fori_loop(0, edge, push, 0)
    for h in range(halves):
        set_ref[:, pl.ds(h * lanes, lanes)] = native_a[h]
        ben_ref[:, pl.ds(h * lanes, lanes)] = native_b[h]

    o_ref[...] = step_ref[...]
    wide = iota((edge, lanes), 1)
    for g in range(groups):
        for s in range(per):
            n = g * per + s
            ax, ay, az = corners[n, 0], corners[n, 1], corners[n, 2]
            turn = lax.rem(az + lanes - s * edge, lanes)
            inside = jnp.logical_and(wide >= az, wide < az + edge)

            def deposit(i, carry, g=g, ax=ax, ay=ay, turn=turn, inside=inside):
                for c in range(3):
                    block = pltpu.roll(force[c, i, pl.ds(g * edge, edge), :], turn, 1)
                    at = (c, ax + i, pl.ds(ay, edge), slice(None))
                    o_ref[at] = o_ref[at] + jnp.where(inside, block, 0.0)
                return carry

            lax.fori_loop(0, edge, deposit, 0, unroll=2)


def bubbles(velocity, box_level, corners, owner_list, stepped):
    slots, edge, plane = box_level.shape
    lanes = velocity.shape[3]
    rows = slots * edge * plane // (edge * lanes)
    flat = (slots * edge, plane)
    f32 = jnp.float32
    whole = pl.BlockSpec(memory_space=pltpu.VMEM)
    smem = pl.BlockSpec(memory_space=pltpu.SMEM)
    field = pltpu.VMEM((edge, rows, lanes), f32)
    triple = pltpu.VMEM((3, edge, rows, lanes), f32)
    native = pltpu.VMEM((plane // lanes, slots * edge, lanes), f32)
    result, settled, bending = pl.pallas_call(
        bubble_kernel,
        out_shape=(
            jax.ShapeDtypeStruct(velocity.shape, f32),
            jax.ShapeDtypeStruct(flat, f32),
            jax.ShapeDtypeStruct(flat, f32),
        ),
        in_specs=[smem, smem, whole, whole, whole],
        out_specs=(whole, whole, whole),
        scratch_shapes=[field, triple, field, field, field, triple, field, field, native, native],
    )(corners, owner_list, velocity, box_level.reshape(flat), stepped)
    return result, settled.reshape(box_level.shape), bending.reshape(box_level.shape)


def local(velocity, box_level, corners, owner_list):
    stepped = momentum(velocity)
    return bubbles(velocity, box_level, corners, owner_list, stepped)


def solution(mesh):
    placed = (
        P(None, "gx", "gy", "gz"),
        P(("gx", "gy", "gz"), None, None),
        P(("gx", "gy", "gz"), None),
        P(("gx", "gy", "gz")),
    )
    return jax.shard_map(
        local,
        mesh=mesh,
        in_specs=placed,
        out_specs=(
            P(None, "gx", "gy", "gz"),
            P(("gx", "gy", "gz"), None, None),
            P(("gx", "gy", "gz"), None, None),
        ),
        check_vma=False,
    )
```

time: 755 us -> 64.4 us (0.09)
  local copies, waits for them, and re-layouts: 442 us -> 1.35 us
  loops' own time: 181 us -> 0 us
  other arithmetic: 107 us -> 0 us
  Pallas kernels: 0 us -> 62.2 us
  starting transfers between devices: 14.7 us -> 0 us
    dynamic_update_slice x16 -> x0, local copies, waits for them, and re-layouts: 320 us -> none  [deposit_slot(): lax.dynamic_update_slice(grid_now, region + grid_step * push_boxes[slot_n...]
    another operation x3 -> x0, loops' own time: 181 us -> none  [the longest x1 90.3 us: local(): result = lax.fori_loop(0, slot_count, deposit_slot, stepped)]
    pallas_call x0 -> x2, Pallas kernels: none -> 62.2 us  [the longest x1 37.6 us: bubbles(): pl.pallas_call(bubble_kernel, out_shape=(jax.ShapeDtypeStruct(velocity.sh...]
    dynamic_slice x48 -> x0, local copies, waits for them, and re-layouts: 49.4 us -> none  [the longest x16 23.3 us: deposit_slot(): corners[slot_no, 2]]
    another operation x17 -> x0, other arithmetic: 29 us -> none
    add x17 -> x0, other arithmetic: 28.8 us -> none  [the longest x16 22 us: deposit_slot(): region + grid_step * push_boxes[slot_no]]
    slice x116 -> x0, local copies, waits for them, and re-layouts: 24.1 us -> none  [the longest x3 6.79 us: extended(): leading = lax.slice_in_dim(x, 0, width, axis=dim)]
    another operation x35 -> x0, local copies, waits for them, and re-layouts: 23.7 us -> none
  transfers between devices with their start and end apart: 12 -> 0, of which waited for: 2 -> 0; matrix products, arithmetic and copies ran while one was open for 20% -> 0% of each run, Pallas kernels for 0% -> 0%
where the time goes in v1:
time: 64.4 us; the launch traced here: 64.2 us
  Pallas kernels  62.2 us (97%)
  local copies, waits for them, and re-layouts  1.35 us (2%)
    pallas_call x1, Pallas kernels, bubbles(): pl.pallas_call(bubble_kernel, out_shape=(jax.ShapeDtypeStruct(velocity.sh...  37.6 us
    pallas_call x1, Pallas kernels, momentum(): pl.pallas_call(functools.partial(momentum_kernel, sizes), out_shape=jax.S...  24.6 us
    unnamed x1, local copies, waits for them, and re-layouts  1.35 us

profile of v1, /device:TPU:0, one launch (start us, length us, event | category | flops | bytes accessed | tf_op | source)
XLA Modules:
  0.0 64.2 jit_solution(174674169626004907)
XLA Ops:
  0.6 1.4 %copy.7.corners = s32[16,3]{1,0:T(8,128)} copy(s32[16,3]{0,1:T(4,128)} %param.6) | data formatting | bytes 384 | tf_op args[2]
  2.0 24.6 %shard_map.67.step_ref = f32[3,32,32,128]{3,2,1,0:T(8,128)} custom-call(f32[3,32,32,128]{3,2,1,0:T(8,128)} %v_ref.1), custom_call_target="tpu_custom_call" | custom-call | tf_op jit(solution)/shard_map/pallas_call | solution.py:142
  26.6 37.6 %shard_map.68 = (f32[3,32,32,128]{3,2,1,0:T(8,128)}, f32[256,256]{1,0:T(8,128)}, f32[256,256]{1,0:T(8,128)}) custom-call(s32[16,3]{1,0:T(8,128)} %copy.7.corners, s32[16]{0:T(128)} %owners.1, f32[3,32,32,128]{3,2,1,0:T(8,128)} %v_ref.1, f32[256,256]{1,0:T(8,128)} %bitcast.3, f32[3,32,32,128]{3,2,1,0:T(8,128)} %shard_map.67.step_ref), custom_call_target="tpu_custom_call" | custom-call | tf_op jit(solution)/shard_map/pallas_call | solution.py:369

commit v2 on v1

v2 whole, which is shorter than its diff:
```python
import functools
import math

import jax
import jax.numpy as jnp
from jax import lax
from jax.experimental import pallas as pl
from jax.experimental.pallas import tpu as pltpu
from jax.sharding import PartitionSpec as P

ITERS = 12

box_step = 0.25
pseudo_step = 0.3
weno_floor = 1e-06
band_width = 1.5
tension = 2.0
grid_step = 0.2
viscosity = 0.1
normal_floor = 0.5
tiny = 1.1754944e-38

FETCH, GATHER, ADVECT, SECTION, BEND, PUSH, DEPOSIT = 4, 1, 2, 2, 4, 2, 4

MESH = pl.DeviceIdType.MESH


def iota(shape, dim):
    return lax.broadcasted_iota(jnp.int32, shape, dim)


def blend(a, b, c, e, f):
    s1 = 13.0 / 12.0 * (a - 2.0 * b + c) ** 2 + 0.25 * (a - 4.0 * b + 3.0 * c) ** 2
    s2 = 13.0 / 12.0 * (b - 2.0 * c + e) ** 2 + 0.25 * (b - e) ** 2
    s3 = 13.0 / 12.0 * (c - 2.0 * e + f) ** 2 + 0.25 * (3.0 * c - 4.0 * e + f) ** 2
    a1, a2, a3 = [(weno_floor + s) ** 2 for s in (s1, s2, s3)]
    n1, n2, n3 = 0.1 * (a2 * a3), 0.6 * (a1 * a3), 0.3 * (a1 * a2)
    p1 = a * (1.0 / 3.0) - b * (7.0 / 6.0) + c * (11.0 / 6.0)
    p2 = b * (-1.0 / 6.0) + c * (5.0 / 6.0) + e * (1.0 / 3.0)
    p3 = c * (1.0 / 3.0) + e * (5.0 / 6.0) - f * (1.0 / 6.0)
    return (n1 * p1 + n2 * p2 + n3 * p3) / (n1 + n2 + n3)


class Box:
    def __init__(self, edge, rows, lanes):
        self.edge, self.rows, self.lanes = edge, rows, lanes
        self.row, self.lane = iota((rows, lanes), 0), iota((rows, lanes), 1)
        j_at, k_at = self.row % edge, self.lane % edge
        self.j_first, self.j_last = j_at == 0, j_at == edge - 1
        self.k_first, self.k_last = k_at == 0, k_at == edge - 1
        self.groups = rows // edge
        self.per = lanes // edge
        self.halves = edge // 8

    def prev_j(self, x):
        return jnp.where(self.j_first, x, pltpu.roll(x, 1, 0))

    def next_j(self, x):
        return jnp.where(self.j_last, x, pltpu.roll(x, self.rows - 1, 0))

    def prev_k(self, x):
        return jnp.where(self.k_first, x, pltpu.roll(x, 1, 1))

    def next_k(self, x):
        return jnp.where(self.k_last, x, pltpu.roll(x, self.lanes - 1, 1))

    def swap_blocks(self, x):
        block = self.lane // self.edge
        for b in (1, 2, 4):
            low = jnp.logical_and((self.row & b) != 0, (block & b) == 0)
            high = jnp.logical_and((self.row & b) == 0, (block & b) != 0)
            down = pltpu.roll(pltpu.roll(x, b, 0), self.lanes - self.edge * b, 1)
            up = pltpu.roll(pltpu.roll(x, self.rows - b, 0), self.edge * b, 1)
            x = jnp.where(low, down, jnp.where(high, up, x))
        return x


def fetch_levels(box, lev_ref, native, lev):
    edge, per, lanes = box.edge, box.per, box.lanes
    for h in range(box.halves):
        native[h] = lev_ref[:, pl.ds(h * lanes, lanes)]

    def fetch(i, carry):
        pieces = [
            native[h, pl.ds(g * per * edge + i, per, stride=edge), :]
            for g in range(box.groups)
            for h in range(box.halves)
        ]
        lev[i] = box.swap_blocks(jnp.concatenate(pieces, axis=0))
        return carry

    lax.fori_loop(0, edge, fetch, 0, unroll=FETCH)


def gather_motion(box, corners, v_ref, mot):
    edge, per, lanes = box.edge, box.per, box.lanes
    slot_lane = iota((edge, lanes), 1) // edge
    for g in range(box.groups):
        places = [[corners[d, g * per + s] for d in range(3)] for s in range(per)]
        turns = [lax.rem(s * edge + lanes - places[s][2], lanes) for s in range(per)]

        def gather(i, carry, g=g, places=places, turns=turns):
            for c in range(3):
                acc = jnp.zeros((edge, lanes), jnp.float32)
                for s in range(per):
                    block = v_ref[c, places[s][0] + i, pl.ds(places[s][1], edge), :]
                    acc = jnp.where(slot_lane == s, pltpu.roll(block, turns[s], 1), acc)
                mot[c, i, pl.ds(g * edge, edge), :] = acc
            return carry

        lax.fori_loop(0, edge, gather, 0, unroll=GATHER)


def advect_levels(box, lev, slope, mot, psa, gain):
    edge = box.edge

    def rise(i, carry):
        slope[i + 3] = lev[i + 1] - lev[i]
        return carry

    zero = jnp.zeros_like(lev[0])
    for n in range(3):
        slope[n] = zero
    lax.fori_loop(0, edge - 1, rise, 0, unroll=5)
    for n in range(3):
        slope[edge + 2 + n] = slope[edge + 1]

    def advect(i, carry):
        here = lev[i]
        change = jnp.zeros_like(here)
        for d in range(3):
            if d == 0:
                slopes = [slope[i + n] for n in range(6)]
            else:
                back, ahead = (box.prev_j, box.next_j) if d == 1 else (box.prev_k, box.next_k)
                mid = here - back(here)
                b1 = back(mid)
                f1 = ahead(mid)
                f2 = ahead(f1)
                slopes = [back(b1), b1, mid, f1, f2, ahead(f2)]
            speed = mot[d, i]
            pos = speed > 0.0
            picks = [jnp.where(pos, slopes[n], slopes[5 - n]) for n in range(5)]
            change = change + speed * blend(*picks)
        out = here - box_step * change
        psa[i] = out
        gain[i] = pseudo_step * out * lax.rsqrt(out * out + 1.0)
        return carry

    lax.fori_loop(0, edge, advect, 0, unroll=ADVECT)


def reinitialize(box, psa, psb, gain):
    edge = box.edge

    def sweep(src, dst):
        for i in range(edge):
            cur = src[i]
            rate = gain[i]
            sign = jnp.where(rate > 0.0, 1.0, -1.0)
            signed = sign * cur
            total = None
            for lo, hi in (
                (src[max(i - 1, 0)], src[min(i + 1, edge - 1)]),
                (box.prev_j(cur), box.next_j(cur)),
                (box.prev_k(cur), box.next_k(cur)),
            ):
                rise = jnp.maximum(signed - jnp.minimum(sign * lo, sign * hi), 0.0)
                total = rise * rise if total is None else total + rise * rise
            root = total * lax.rsqrt(jnp.maximum(total, tiny))
            dst[i] = cur - rate * (root - 1.0)

    def two_sweeps(n, carry):
        sweep(psa, psb)
        sweep(psb, psa)
        return carry

    lax.fori_loop(0, ITERS // 2, two_sweeps, 0)


def pack_z(src, dst, xs, ys, lanes):
    group = iota((ys, lanes), 1) // 4

    def step(x, accs):
        shift = 4 * x + 1
        return tuple(
            jnp.where(group == x, pltpu.roll(src[c, x], shift, 1), accs[c]) for c in range(3)
        )

    accs = lax.fori_loop(
        0, xs, step, tuple(jnp.zeros((ys, lanes), jnp.float32) for _ in range(3)), unroll=8
    )
    for c in range(3):
        dst[c] = accs[c]


def step_kernel(
    sizes, corners, v_hbm, lev_ref, o_ref, psi_ref,
    vel, pred, xrecv, ysend, yrecv, zsend, zrecv, comb, lev, slope, mot, psb, gain, native,
    local_sem, send_sem, recv_sem,
):
    _, xs, ys, lanes = v_hbm.shape
    box = Box(*lev.shape)
    load = pltpu.make_async_copy(v_hbm, vel, local_sem)
    load.start()
    ups, downs = [], []
    for axis in ("gx", "gy", "gz"):
        me, n = lax.axis_index(axis), sizes[axis]
        ups.append({axis: lax.rem(me + 1, n)})
        downs.append({axis: lax.rem(me + n - 1, n)})
    barrier = pltpu.get_barrier_semaphore()
    for target in ups + downs:
        pl.semaphore_signal(barrier, inc=1, device_id=target, device_id_type=MESH)
    fetch_levels(box, lev_ref, native, lev)
    load.wait()

    def pack(r, src):
        for c in range(3):
            ysend[r, 0, c] = src[c, :, ys - 1, :]
            ysend[r, 1, c] = src[c, :, 0, :]
        pack_z(src, zsend.at[r], xs, ys, lanes)

    def exchange(r, src):
        copies = []

        def send(n, src, dst, target):
            copy = pltpu.make_async_remote_copy(
                src_ref=src,
                dst_ref=dst,
                send_sem=send_sem.at[r, n],
                recv_sem=recv_sem.at[r, n],
                device_id=target,
                device_id_type=MESH,
            )
            copy.start()
            copies.append(copy)

        send(0, src.at[:, xs - 1], xrecv.at[r, 0], ups[0])
        send(1, src.at[:, 0], xrecv.at[r, 1], downs[0])
        send(2, ysend.at[r, 0], yrecv.at[r, 0], ups[1])
        send(3, ysend.at[r, 1], yrecv.at[r, 1], downs[1])
        send(4, zsend.at[r], zrecv.at[r, 0], ups[2])
        send(5, zsend.at[r], zrecv.at[r, 1], downs[2])
        return copies

    lane = iota((ys, lanes), 1)
    row = iota((ys, lanes), 0)
    quarter = lane % 4

    def section(r, src, emit):
        for c in range(3):
            comb[c] = jnp.where(
                quarter == 0,
                pltpu.roll(zrecv[r, 1, c], lanes - 1, 1),
                pltpu.roll(zrecv[r, 0, c], 1, 1),
            )

        def plane(x, before, after):
            centre = [src[c, x] for c in range(3)]
            for c in range(3):
                mid = centre[c]
                x_lo, x_hi = before(c), after(c)
                y_lo = jnp.where(row == 0, yrecv[r, 0, c, pl.ds(x, 1), :], pltpu.roll(mid, 1, 0))
                y_hi = jnp.where(
                    row == ys - 1, yrecv[r, 1, c, pl.ds(x, 1), :], pltpu.roll(mid, ys - 1, 0)
                )
                halo = pltpu.roll(comb[c], lanes - 1 - 4 * x, 1)
                z_lo = jnp.where(lane == 0, halo, pltpu.roll(mid, 1, 1))
                z_hi = jnp.where(lane == lanes - 1, halo, pltpu.roll(mid, lanes - 1, 1))
                spread = (x_hi + x_lo) + (y_hi + y_lo) + (z_hi + z_lo) - 6.0 * mid
                advect = (
                    centre[0] * (x_hi - x_lo) + centre[1] * (y_hi - y_lo) + centre[2] * (z_hi - z_lo)
                )
                emit(c, x, mid + grid_step * (viscosity * spread - 0.5 * advect))

        def step(x, carry):
            plane(x, lambda c: src[c, x - 1], lambda c: src[c, x + 1])
            return carry

        plane(0, lambda c: xrecv[r, 0, c], lambda c: src[c, 1])
        lax.fori_loop(1, xs - 1, step, 0, unroll=SECTION)
        plane(xs - 1, lambda c: src[c, xs - 2], lambda c: xrecv[r, 1, c])

    def first(c, x, value):
        pred[c, x] = value

    def second(c, x, value):
        o_ref[c, x] = 0.5 * (vel[c, x] + value)

    pack(0, vel)
    pl.semaphore_wait(barrier, 6)
    copies = exchange(0, vel)
    gather_motion(box, corners, vel, mot)
    advect_levels(box, lev, slope, mot, psi_ref, gain)
    for copy in copies:
        copy.wait()
    section(0, vel, first)
    pack(1, pred)
    copies = exchange(1, pred)
    reinitialize(box, psi_ref, psb, gain)
    for copy in copies:
        copy.wait()
    section(1, pred, second)


def step_call(velocity, box_level, corners):
    sizes = {axis: lax.axis_size(axis) for axis in ("gx", "gy", "gz")}
    _, xs, ys, lanes = velocity.shape
    slots, edge, plane = box_level.shape
    rows = slots * edge * plane // (edge * lanes)
    vmem = pltpu.VMEM
    f32 = jnp.float32
    whole = pl.BlockSpec(memory_space=pltpu.VMEM)
    return pl.pallas_call(
        functools.partial(step_kernel, sizes),
        out_shape=(
            jax.ShapeDtypeStruct(velocity.shape, f32),
            jax.ShapeDtypeStruct((edge, rows, lanes), f32),
        ),
        in_specs=[
            pl.BlockSpec(memory_space=pltpu.SMEM),
            pl.BlockSpec(memory_space=pl.ANY),
            whole,
        ],
        out_specs=(whole, whole),
        scratch_shapes=[
            vmem(velocity.shape, f32),
            vmem(velocity.shape, f32),
            vmem((2, 2, 3, ys, lanes), f32),
            vmem((2, 2, 3, xs, lanes), f32),
            vmem((2, 2, 3, xs, lanes), f32),
            vmem((2, 3, ys, lanes), f32),
            vmem((2, 2, 3, ys, lanes), f32),
            vmem((3, ys, lanes), f32),
            vmem((edge, rows, lanes), f32),
            vmem((edge + 5, rows, lanes), f32),
            vmem((3, edge, rows, lanes), f32),
            vmem((edge, rows, lanes), f32),
            vmem((edge, rows, lanes), f32),
            vmem((plane // lanes, slots * edge, lanes), f32),
            pltpu.SemaphoreType.DMA(()),
            pltpu.SemaphoreType.DMA((2, 6)),
            pltpu.SemaphoreType.DMA((2, 6)),
        ],
        compiler_params=pltpu.CompilerParams(collective_id=0, has_side_effects=True),
    )(corners, velocity, box_level.reshape(slots * edge, plane))


def force_kernel(
    corners, owners, psi, step_hbm, o_ref, set_ref, ben_ref, force, part, nrm, native_a, native_b, sem
):
    load = pltpu.make_async_copy(step_hbm, o_ref, sem)
    load.start()
    box = Box(*psi.shape)
    edge, per, groups, lanes = box.edge, box.per, box.groups, box.lanes

    def write(ref, i, value):
        value = box.swap_blocks(value)
        for g in range(groups):
            for h in range(box.halves):
                at = g * edge + h * 8
                ref[h, pl.ds(g * per * edge + i, per, stride=edge), :] = value[at : at + 8]

    alive = jnp.zeros((box.rows, lanes), jnp.float32)
    owner_at = (box.row // edge) * per + box.lane // edge
    for s in range(groups * per):
        alive = jnp.where(owner_at == s, jnp.where(owners[s] >= 0, 1.0, 0.0), alive)

    def bend(i, carry):
        cur = psi[i]
        c0 = 0.5 * (psi[jnp.minimum(i + 1, edge - 1)] - psi[jnp.maximum(i - 1, 0)])
        c1 = 0.5 * (box.next_j(cur) - box.prev_j(cur))
        c2 = 0.5 * (box.next_k(cur) - box.prev_k(cur))
        inverse = lax.rsqrt(jnp.maximum(c0 * c0 + c1 * c1 + c2 * c2, normal_floor * normal_floor))
        n1, n2 = c1 * inverse, c2 * inverse
        nrm[i] = c0 * inverse
        part[i] = 0.5 * (box.next_j(n1) - box.prev_j(n1)) + 0.5 * (box.next_k(n2) - box.prev_k(n2))
        force[0, i] = c0
        force[1, i] = c1
        force[2, i] = c2
        return carry

    lax.fori_loop(0, edge, bend, 0, unroll=BEND)

    def push(i, carry):
        level = psi[i] * alive
        curve = (
            part[i] + 0.5 * (nrm[jnp.minimum(i + 1, edge - 1)] - nrm[jnp.maximum(i - 1, 0)])
        ) * alive
        write(native_a, i, level)
        write(native_b, i, curve)
        ratio = level * (1.0 / band_width)
        scale = grid_step * tension / (band_width * math.sqrt(math.pi))
        strength = scale * curve * jnp.exp(-(ratio * ratio)) * alive
        for d in range(3):
            force[d, i] = force[d, i] * strength
        return carry

    lax.fori_loop(0, edge, push, 0, unroll=PUSH)
    for h in range(box.halves):
        set_ref[:, pl.ds(h * lanes, lanes)] = native_a[h]
        ben_ref[:, pl.ds(h * lanes, lanes)] = native_b[h]

    load.wait()
    wide = iota((edge, lanes), 1)

    def deposit_slot(n, carry):
        g, s = n // per, n % per
        ax, ay, az = corners[0, n], corners[1, n], corners[2, n]
        turn = lax.rem(az + lanes - s * edge, lanes)
        inside = jnp.logical_and(wide >= az, wide < az + edge)
        first_row = pl.multiple_of(g * edge, edge)

        for i in range(0, edge, DEPOSIT):
            spots = [(c, i + t) for t in range(DEPOSIT) for c in range(3)]
            blocks = [pltpu.roll(force[c, q, pl.ds(first_row, edge), :], turn, 1) for c, q in spots]
            olds = [o_ref[c, ax + q, pl.ds(ay, edge), :] for c, q in spots]
            news = [old + jnp.where(inside, block, 0.0) for old, block in zip(olds, blocks)]
            for (c, q), new in zip(spots, news):
                o_ref[c, ax + q, pl.ds(ay, edge), :] = new
        return carry

    lax.fori_loop(0, groups * per, deposit_slot, 0)


def force_call(shapes, psi, corners, owner_list, stepped):
    slots, edge, plane = shapes
    rows, lanes = psi.shape[1:]
    flat = (slots * edge, plane)
    f32 = jnp.float32
    whole = pl.BlockSpec(memory_space=pltpu.VMEM)
    smem = pl.BlockSpec(memory_space=pltpu.SMEM)
    field = pltpu.VMEM((edge, rows, lanes), f32)
    native = pltpu.VMEM((plane // lanes, slots * edge, lanes), f32)
    result, settled, bending = pl.pallas_call(
        force_kernel,
        out_shape=(
            jax.ShapeDtypeStruct(stepped.shape, f32),
            jax.ShapeDtypeStruct(flat, f32),
            jax.ShapeDtypeStruct(flat, f32),
        ),
        in_specs=[smem, smem, whole, pl.BlockSpec(memory_space=pl.ANY)],
        out_specs=(whole, whole, whole),
        scratch_shapes=[
            pltpu.VMEM((3, edge, rows, lanes), f32),
            field,
            field,
            native,
            native,
            pltpu.SemaphoreType.DMA(()),
        ],
    )(corners, owner_list, psi, stepped)
    return result, settled.reshape(shapes), bending.reshape(shapes)


def local(velocity, box_level, corners, owner_list):
    turned = corners.T
    stepped, psi = step_call(velocity, box_level, turned)
    return force_call(box_level.shape, psi, turned, owner_list, stepped)


def solution(mesh):
    placed = (
        P(None, "gx", "gy", "gz"),
        P(("gx", "gy", "gz"), None, None),
        P(("gx", "gy", "gz"), None),
        P(("gx", "gy", "gz")),
    )
    return jax.shard_map(
        local,
        mesh=mesh,
        in_specs=placed,
        out_specs=(
            P(None, "gx", "gy", "gz"),
            P(("gx", "gy", "gz"), None, None),
            P(("gx", "gy", "gz"), None, None),
        ),
        check_vma=False,
    )
```

time: 64.4 us -> 34.4 us (0.53)
  Pallas kernels: 62.2 us -> 33.6 us
  local copies, waits for them, and re-layouts: 1.35 us -> 0 us
    pallas_call x2, Pallas kernels: 62.2 us -> 33.6 us  [the longest x1 25.5 us: step_call(): pl.pallas_call(functools.partial(step_kernel, sizes), out_shape=(jax.Shap...]
    unnamed x1 -> x0, local copies, waits for them, and re-layouts: 1.35 us -> none
where the time goes in v2:
time: 34.4 us; the launch traced here: 34.2 us
  Pallas kernels  33.6 us (98%)
  between operations  0.64 us (2%)
    pallas_call x1, Pallas kernels, step_call(): pl.pallas_call(functools.partial(step_kernel, sizes), out_shape=(jax.Shap...  25.5 us
    pallas_call x1, Pallas kernels, force_call(): pl.pallas_call(force_kernel, out_shape=(jax.ShapeDtypeStruct(stepped.shap...  8.06 us

profile of v2, /device:TPU:0, one launch (start us, length us, event | category | flops | bytes accessed | tf_op | source)
XLA Modules:
  0.0 34.2 jit_solution(14966552079144417027)
XLA Ops:
  0.6 25.5 %shard_map.67 = (f32[3,32,32,128]{3,2,1,0:T(8,128)}, f32[16,32,128]{2,1,0:T(8,128)}) custom-call(s32[3,16]{1,0:T(4,128)} %bitcast.5, f32[3,32,32,128]{3,2,1,0:T(8,128)} %v_hbm.1, f32[256,256]{1,0:T(8,128)} %bitcast.4), custom_call_target="tpu_custom_call" | custom-call | tf_op jit(solution)/shard_map/pallas_call | solution.py:314
  26.2 8.1 %shard_map.68 = (f32[3,32,32,128]{3,2,1,0:T(8,128)}, f32[256,256]{1,0:T(8,128)}, f32[256,256]{1,0:T(8,128)}) custom-call(s32[3,16]{1,0:T(4,128)} %bitcast.6, s32[16]{0:T(128)} %owners.1, f32[16,32,128]{2,1,0:T(8,128)} %get-tuple-element.8.psi, f32[3,32,32,128]{3,2,1,0:T(8,128)} %get-tuple-element.9.step_hbm), custom_call_target="tpu_custom_call" | custom-call | tf_op jit(solution)/shard_map/pallas_call | solution.py:435

commit v3 on v2

--- a/solution.py
+++ b/solution.py
@@ -20,7 +20,7 @@
 normal_floor = 0.5
 tiny = 1.1754944e-38
 
-FETCH, GATHER, ADVECT, SECTION, BEND, PUSH, DEPOSIT = 4, 1, 2, 2, 4, 2, 4
+FETCH, GATHER, ADVECT, SECTION, BEND, PUSH, DEPOSIT = 4, 2, 4, 5, 4, 4, 4
 
 MESH = pl.DeviceIdType.MESH
 
@@ -30,15 +30,19 @@
 
 
 def blend(a, b, c, e, f):
-    s1 = 13.0 / 12.0 * (a - 2.0 * b + c) ** 2 + 0.25 * (a - 4.0 * b + 3.0 * c) ** 2
-    s2 = 13.0 / 12.0 * (b - 2.0 * c + e) ** 2 + 0.25 * (b - e) ** 2
-    s3 = 13.0 / 12.0 * (c - 2.0 * e + f) ** 2 + 0.25 * (3.0 * c - 4.0 * e + f) ** 2
-    a1, a2, a3 = [(weno_floor + s) ** 2 for s in (s1, s2, s3)]
-    n1, n2, n3 = 0.1 * (a2 * a3), 0.6 * (a1 * a3), 0.3 * (a1 * a2)
-    p1 = a * (1.0 / 3.0) - b * (7.0 / 6.0) + c * (11.0 / 6.0)
-    p2 = b * (-1.0 / 6.0) + c * (5.0 / 6.0) + e * (1.0 / 3.0)
-    p3 = c * (1.0 / 3.0) + e * (5.0 / 6.0) - f * (1.0 / 6.0)
-    return (n1 * p1 + n2 * p2 + n3 * p3) / (n1 + n2 + n3)
+    d1, d2, d3, d4 = a - b, b - c, c - e, e - f
+    twice, thrice = 3.0 * d2, 3.0 * d3
+    x1, x2, x3 = d1 - d2, d2 - d3, d3 - d4
+    y1, y2, y3 = d1 - twice, d2 + d3, thrice - d4
+    a1, a2, a3 = [
+        (4.0 * weno_floor + (y * y + 13.0 / 3.0 * (x * x))) ** 2
+        for x, y in ((x1, y1), (x2, y2), (x3, y3))
+    ]
+    n1, n2, n3 = a2 * a3, a1 * (6.0 * a3), a1 * (3.0 * a2)
+    q1 = 2.0 * d1 - 5.0 * d2
+    q2 = d2 + 2.0 * d3
+    q3 = d4 - 4.0 * d3
+    return c + (n1 * q1 - n2 * q2 + n3 * q3) / (6.0 * (n1 + n2 + n3))
 
 
 class Box:
@@ -195,9 +199,9 @@
 
 
 def step_kernel(
-    sizes, corners, v_hbm, lev_ref, o_ref, psi_ref,
-    vel, pred, xrecv, ysend, yrecv, zsend, zrecv, comb, lev, slope, mot, psb, gain, native,
-    local_sem, send_sem, recv_sem,
+    sizes, corners, v_hbm, lev_ref, o_hbm, psi_ref,
+    vel, out, pred, xrecv, ysend, yrecv, zsend, zrecv, comb, lev, slope, mot, psb, gain, native,
+    local_sem, out_sem, send_sem, recv_sem,
 ):
     _, xs, ys, lanes = v_hbm.shape
     box = Box(*lev.shape)
@@ -247,7 +251,13 @@
     row = iota((ys, lanes), 0)
     quarter = lane % 4
 
-    def section(r, src, emit):
+    half = xs // 2
+
+    def store(n):
+        part = pl.ds(n * half, half)
+        return pltpu.make_async_copy(out.at[:, part], o_hbm.at[:, part], out_sem.at[n])
+
+    def section(r, src, emit, done):
         for c in range(3):
             comb[c] = jnp.where(
                 quarter == 0,
@@ -278,14 +288,17 @@
             return carry
 
         plane(0, lambda c: xrecv[r, 0, c], lambda c: src[c, 1])
-        lax.fori_loop(1, xs - 1, step, 0, unroll=SECTION)
+        lax.fori_loop(1, half, step, 0, unroll=SECTION)
+        done(0)
+        lax.fori_loop(half, xs - 1, step, 0, unroll=SECTION)
         plane(xs - 1, lambda c: src[c, xs - 2], lambda c: xrecv[r, 1, c])
+        done(1)
 
     def first(c, x, value):
         pred[c, x] = value
 
     def second(c, x, value):
-        o_ref[c, x] = 0.5 * (vel[c, x] + value)
+        out[c, x] = 0.5 * (vel[c, x] + value)
 
     pack(0, vel)
     pl.semaphore_wait(barrier, 6)
@@ -294,13 +307,15 @@
     advect_levels(box, lev, slope, mot, psi_ref, gain)
     for copy in copies:
         copy.wait()
-    section(0, vel, first)
+    section(0, vel, first, lambda n: None)
     pack(1, pred)
     copies = exchange(1, pred)
     reinitialize(box, psi_ref, psb, gain)
     for copy in copies:
         copy.wait()
-    section(1, pred, second)
+    section(1, pred, second, lambda n: store(n).start())
+    store(0).wait()
+    store(1).wait()
 
 
 def step_call(velocity, box_level, corners):
@@ -322,8 +337,9 @@
             pl.BlockSpec(memory_space=pl.ANY),
             whole,
         ],
-        out_specs=(whole, whole),
+        out_specs=(pl.BlockSpec(memory_space=pl.ANY), whole),
         scratch_shapes=[
+            vmem(velocity.shape, f32),
             vmem(velocity.shape, f32),
             vmem(velocity.shape, f32),
             vmem((2, 2, 3, ys, lanes), f32),
@@ -339,6 +355,7 @@
             vmem((edge, rows, lanes), f32),
             vmem((plane // lanes, slots * edge, lanes), f32),
             pltpu.SemaphoreType.DMA(()),
+            pltpu.SemaphoreType.DMA((2,)),
             pltpu.SemaphoreType.DMA((2, 6)),
             pltpu.SemaphoreType.DMA((2, 6)),
         ],

time: 34.4 us -> 30.5 us (0.89)
  Pallas kernels: 33.6 us -> 29.7 us
    pallas_call x1, Pallas kernels: 25.5 us -> 22.4 us  [step_call(): pl.pallas_call(functools.partial(step_kernel, sizes), out_shape=(jax.Shap...]
    pallas_call x1, Pallas kernels: 8.06 us -> 7.33 us  [force_call(): pl.pallas_call(force_kernel, out_shape=(jax.ShapeDtypeStruct(stepped.shap...]
where the time goes in v3:
time: 30.5 us; the launch traced here: 30.3 us
  Pallas kernels  29.7 us (97%)
  between operations  0.64 us (2%)
    pallas_call x1, Pallas kernels, step_call(): pl.pallas_call(functools.partial(step_kernel, sizes), out_shape=(jax.Shap...  22.4 us
    pallas_call x1, Pallas kernels, force_call(): pl.pallas_call(force_kernel, out_shape=(jax.ShapeDtypeStruct(stepped.shap...  7.33 us

profile of v3, /device:TPU:0, one launch (start us, length us, event | category | flops | bytes accessed | tf_op | source)
XLA Modules:
  0.0 30.3 jit_solution(8153806862633386275)
XLA Ops:
  0.6 22.4 %shard_map.67 = (f32[3,32,32,128]{3,2,1,0:T(8,128)}, f32[16,32,128]{2,1,0:T(8,128)}) custom-call(s32[3,16]{1,0:T(4,128)} %bitcast.5, f32[3,32,32,128]{3,2,1,0:T(8,128)} %v_hbm.1, f32[256,256]{1,0:T(8,128)} %bitcast.4), custom_call_target="tpu_custom_call" | custom-call | tf_op jit(solution)/shard_map/pallas_call | solution.py:329
  23.0 7.3 %shard_map.68 = (f32[3,32,32,128]{3,2,1,0:T(8,128)}, f32[256,256]{1,0:T(8,128)}, f32[256,256]{1,0:T(8,128)}) custom-call(s32[3,16]{1,0:T(4,128)} %bitcast.6, s32[16]{0:T(128)} %owners.1, f32[16,32,128]{2,1,0:T(8,128)} %get-tuple-element.8.psi, f32[3,32,32,128]{3,2,1,0:T(8,128)} %get-tuple-element.9.step_hbm), custom_call_target="tpu_custom_call" | custom-call | tf_op jit(solution)/shard_map/pallas_call | solution.py:452

commit v4 on v3

--- a/solution.py
+++ b/solution.py
@@ -79,10 +79,8 @@
         return x
 
 
-def fetch_levels(box, lev_ref, native, lev):
-    edge, per, lanes = box.edge, box.per, box.lanes
-    for h in range(box.halves):
-        native[h] = lev_ref[:, pl.ds(h * lanes, lanes)]
+def fetch_levels(box, native, lev):
+    edge, per = box.edge, box.per
 
     def fetch(i, carry):
         pieces = [
@@ -199,12 +197,18 @@
 
 
 def step_kernel(
-    sizes, corners, v_hbm, lev_ref, o_hbm, psi_ref,
-    vel, out, pred, xrecv, ysend, yrecv, zsend, zrecv, comb, lev, slope, mot, psb, gain, native,
-    local_sem, out_sem, send_sem, recv_sem,
+    sizes, corners, v_hbm, lev_hbm, o_hbm, psi_hbm,
+    vel, out, psi_ref, pred, xrecv, ysend, yrecv, zsend, zrecv, comb, lev, slope, mot, psb, gain, native,
+    local_sem, lev_sem, out_sem, psi_sem, send_sem, recv_sem,
 ):
     _, xs, ys, lanes = v_hbm.shape
     box = Box(*lev.shape)
+    levels = [
+        pltpu.make_async_copy(lev_hbm.at[:, pl.ds(h * lanes, lanes)], native.at[h], lev_sem.at[h])
+        for h in range(box.halves)
+    ]
+    for part in levels:
+        part.start()
     load = pltpu.make_async_copy(v_hbm, vel, local_sem)
     load.start()
     ups, downs = [], []
@@ -215,7 +219,9 @@
     barrier = pltpu.get_barrier_semaphore()
     for target in ups + downs:
         pl.semaphore_signal(barrier, inc=1, device_id=target, device_id_type=MESH)
-    fetch_levels(box, lev_ref, native, lev)
+    for part in levels:
+        part.wait()
+    fetch_levels(box, native, lev)
     load.wait()
 
     def pack(r, src):
@@ -311,11 +317,14 @@
     pack(1, pred)
     copies = exchange(1, pred)
     reinitialize(box, psi_ref, psb, gain)
+    keep = pltpu.make_async_copy(psi_ref, psi_hbm, psi_sem)
+    keep.start()
     for copy in copies:
         copy.wait()
     section(1, pred, second, lambda n: store(n).start())
     store(0).wait()
     store(1).wait()
+    keep.wait()
 
 
 def step_call(velocity, box_level, corners):
@@ -325,7 +334,6 @@
     rows = slots * edge * plane // (edge * lanes)
     vmem = pltpu.VMEM
     f32 = jnp.float32
-    whole = pl.BlockSpec(memory_space=pltpu.VMEM)
     return pl.pallas_call(
         functools.partial(step_kernel, sizes),
         out_shape=(
@@ -335,12 +343,13 @@
         in_specs=[
             pl.BlockSpec(memory_space=pltpu.SMEM),
             pl.BlockSpec(memory_space=pl.ANY),
-            whole,
+            pl.BlockSpec(memory_space=pl.ANY),
         ],
-        out_specs=(pl.BlockSpec(memory_space=pl.ANY), whole),
+        out_specs=(pl.BlockSpec(memory_space=pl.ANY), pl.BlockSpec(memory_space=pl.ANY)),
         scratch_shapes=[
             vmem(velocity.shape, f32),
             vmem(velocity.shape, f32),
+            vmem((edge, rows, lanes), f32),
             vmem(velocity.shape, f32),
             vmem((2, 2, 3, ys, lanes), f32),
             vmem((2, 2, 3, xs, lanes), f32),
@@ -355,7 +364,9 @@
             vmem((edge, rows, lanes), f32),
             vmem((plane // lanes, slots * edge, lanes), f32),
             pltpu.SemaphoreType.DMA(()),
+            pltpu.SemaphoreType.DMA((plane // lanes,)),
             pltpu.SemaphoreType.DMA((2,)),
+            pltpu.SemaphoreType.DMA(()),
             pltpu.SemaphoreType.DMA((2, 6)),
             pltpu.SemaphoreType.DMA((2, 6)),
         ],
@@ -364,7 +375,8 @@
 
 
 def force_kernel(
-    corners, owners, psi, step_hbm, o_ref, set_ref, ben_ref, force, part, nrm, native_a, native_b, sem
+    corners, owners, psi, step_hbm, o_hbm, set_hbm, ben_hbm,
+    o_ref, force, part, nrm, native_a, native_b, sem, out_sem, small_sem,
 ):
     load = pltpu.make_async_copy(step_hbm, o_ref, sem)
     load.start()
@@ -414,9 +426,13 @@
         return carry
 
     lax.fori_loop(0, edge, push, 0, unroll=PUSH)
+    stores = []
     for h in range(box.halves):
-        set_ref[:, pl.ds(h * lanes, lanes)] = native_a[h]
-        ben_ref[:, pl.ds(h * lanes, lanes)] = native_b[h]
+        part_h = pl.ds(h * lanes, lanes)
+        stores.append(pltpu.make_async_copy(native_a.at[h], set_hbm.at[:, part_h], small_sem.at[0, h]))
+        stores.append(pltpu.make_async_copy(native_b.at[h], ben_hbm.at[:, part_h], small_sem.at[1, h]))
+    for copy in stores:
+        copy.start()
 
     load.wait()
     wide = iota((edge, lanes), 1)
@@ -438,6 +454,11 @@
         return carry
 
     lax.fori_loop(0, groups * per, deposit_slot, 0)
+    for c in range(3):
+        stores.append(pltpu.make_async_copy(o_ref.at[c], o_hbm.at[c], out_sem.at[c]))
+        stores[-1].start()
+    for copy in stores:
+        copy.wait()
 
 
 def force_call(shapes, psi, corners, owner_list, stepped):
@@ -457,14 +478,17 @@
             jax.ShapeDtypeStruct(flat, f32),
         ),
         in_specs=[smem, smem, whole, pl.BlockSpec(memory_space=pl.ANY)],
-        out_specs=(whole, whole, whole),
+        out_specs=(pl.BlockSpec(memory_space=pl.ANY),) * 3,
         scratch_shapes=[
+            pltpu.VMEM(stepped.shape, f32),
             pltpu.VMEM((3, edge, rows, lanes), f32),
             field,
             field,
             native,
             native,
             pltpu.SemaphoreType.DMA(()),
+            pltpu.SemaphoreType.DMA((3,)),
+            pltpu.SemaphoreType.DMA((2, plane // lanes)),
         ],
     )(corners, owner_list, psi, stepped)
     return result, settled.reshape(shapes), bending.reshape(shapes)

time: 30.5 us -> 30.2 us (level)
  no operation moved by 1% of the time
where the time goes in v4:
time: 30.2 us; the launch traced here: 30 us
  Pallas kernels  29.4 us (97%)
  between operations  0.64 us (2%)
    pallas_call x1, Pallas kernels, step_call(): pl.pallas_call(functools.partial(step_kernel, sizes), out_shape=(jax.Shap...  22.1 us
    pallas_call x1, Pallas kernels, force_call(): pl.pallas_call(force_kernel, out_shape=(jax.ShapeDtypeStruct(stepped.shap...  7.33 us

profile of v4, /device:TPU:0, one launch (start us, length us, event | category | flops | bytes accessed | tf_op | source)
XLA Modules:
  0.0 30.0 jit_solution(17200234636471305571)
XLA Ops:
  0.6 22.1 %shard_map.67 = (f32[3,32,32,128]{3,2,1,0:T(8,128)}, f32[16,32,128]{2,1,0:T(8,128)}) custom-call(s32[3,16]{1,0:T(4,128)} %bitcast.5, f32[3,32,32,128]{3,2,1,0:T(8,128)} %v_hbm.1, f32[256,256]{1,0:T(8,128)} %bitcast.4), custom_call_target="tpu_custom_call" | custom-call | tf_op jit(solution)/shard_map/pallas_call | solution.py:337
  22.7 7.3 %shard_map.68 = (f32[3,32,32,128]{3,2,1,0:T(8,128)}, f32[256,256]{1,0:T(8,128)}, f32[256,256]{1,0:T(8,128)}) custom-call(s32[3,16]{1,0:T(4,128)} %bitcast.6, s32[16]{0:T(128)} %owners.1, f32[16,32,128]{2,1,0:T(8,128)} %get-tuple-element.8.psi, f32[3,32,32,128]{3,2,1,0:T(8,128)} %get-tuple-element.9.step_hbm), custom_call_target="tpu_custom_call" | custom-call | tf_op jit(solution)/shard_map/pallas_call | solution.py:473
